TPU v7x, 128 devices: a whole 4x4x4 slice. The times are simulated.
128 devices in a mesh: dp: 4 (over z), fsdp: 32 (over y, x, core).
Axes of the slice: x: 4, y: 4, z: 4, core: 2. Of those that a mesh axis runs over, the one named last changes fastest.
Arguments:
- logged: bfloat16 [2048, 8192], P('dp', 'fsdp'), may hold values from -6 to 6
- pairs: int32 [512, 2], P('dp'), may hold values from 0 to 511
- clicks: int32 [512], P('dp'), may hold values 0 or 1
- query_pairs: int32 [32, 2], P('dp'), may hold values from 0 to 511
- query_clicks: int32 [32], P('dp'), may hold values 0 or 1
- first_weight: bfloat16 [8192, 8192], P(None, 'fsdp'), may hold values from -0.0625 to 0.0625
- second_weight: bfloat16 [8192, 8192], P(None, 'fsdp'), may hold values from -0.0625 to 0.0625
- head_weight: float32 [8192], P('fsdp'), may hold values from -0.0625 to 0.0625
Outputs:
- solution: float32 [8192, 8192], P('dp', 'fsdp')
- influence: float32 [512], P('dp')
Inputs may be any that keep to these rules, and one draw needn't show every extreme that they name: Each block of 128 pairs indexes rows within the matching block of 512 logged rows. `query_pairs`: each block of 8 query pairs indexes rows within the matching block of 512 logged rows.
All inputs are finite; a program needn't handle non-finite values. No bound on the sum of `clicks` or of `query_clicks` on one device may be relied on, other than what follows from the above.
Results may differ from a plain program's by a relative error of at most 0.035.
Values may be sent and summed in bfloat16 or wider, within the bound.
A program may use at most 128 MiB of HBM per device.

v0:
```python
import jax
import jax.numpy as jnp
from jax import lax
from jax.sharding import PartitionSpec as P

DAMPING = 0.01


def pair_terms(first_score, second_score, outcome):
    signed = 2.0 * outcome.astype(jnp.float32) - 1.0
    margin = first_score - second_score
    slope_term = -signed * jax.nn.sigmoid(-signed * margin)
    curve_term = jax.nn.sigmoid(signed * margin) * jax.nn.sigmoid(-signed * margin)
    return (slope_term, curve_term)


def solver_total(value):
    return lax.psum(value, ("dp", "fsdp"))


def contract_rows(left, right):
    return lax.dot_general(
        left, right, (((0,), (0,)), ((), ())), preferred_element_type=jnp.float32
    )


def local(
    logged, pairs, clicks, query_pairs, query_clicks, first_weight, second_weight, head_weight
):
    npairs = pairs.shape[0]
    nqueries = query_pairs.shape[0]
    count = 2 * npairs
    row_ids = jnp.concatenate([pairs[:, 0], pairs[:, 1], query_pairs[:, 0], query_pairs[:, 1]])
    local_rows = jnp.take(logged, row_ids, axis=0)
    feats = lax.all_gather(local_rows, "fsdp", axis=1, tiled=True)
    hidden = jnp.tanh(jnp.dot(feats, first_weight, preferred_element_type=jnp.float32)).astype(
        jnp.bfloat16
    )
    second_pre = jnp.dot(
        lax.all_gather(hidden, "fsdp", axis=1, tiled=True),
        second_weight,
        preferred_element_type=jnp.float32,
    )
    output_act = jnp.tanh(second_pre)
    scores_all = lax.psum(jnp.sum(output_act * head_weight, axis=1), "fsdp")
    coef = (head_weight * (1.0 - output_act * output_act)).astype(jnp.bfloat16)
    back_term = lax.dot_general(
        coef, second_weight, (((1,), (1,)), ((), ())), preferred_element_type=jnp.float32
    )
    back = lax.psum_scatter(
        back_term.astype(jnp.bfloat16), "fsdp", scatter_dimension=1, tiled=True
    ).astype(jnp.float32)
    hidden_float = hidden.astype(jnp.float32)
    mixing = (1.0 - hidden_float * hidden_float) * back
    slope_train, curve_train = pair_terms(scores_all[:npairs], scores_all[npairs:count], clicks)
    slope_query = pair_terms(
        scores_all[count : count + nqueries], scores_all[count + nqueries :], query_clicks
    )[0]
    query_err = jnp.concatenate([slope_query, -slope_query])
    query_rows = (query_err[:, None] * mixing[count:]).astype(jnp.bfloat16)
    grad_local = contract_rows(feats[count:], query_rows)
    gradient = lax.psum_scatter(
        grad_local.astype(jnp.bfloat16), "dp", scatter_dimension=0, tiled=True
    ).astype(jnp.float32)
    train_feats = feats[:count]
    train_mix = mixing[:count]

    def apply_curvature(direction):
        packed = direction.astype(jnp.bfloat16)
        gathered = lax.all_gather(packed, "dp", axis=0, tiled=True)
        project = jnp.dot(train_feats, gathered, preferred_element_type=jnp.float32)
        response = lax.psum(jnp.sum(train_mix * project, axis=1), "fsdp")
        rdiff = response[:npairs] - response[npairs:]
        resp_err = jnp.concatenate([curve_train * rdiff, -curve_train * rdiff])
        resp_rows = (resp_err[:, None] * train_mix).astype(jnp.bfloat16)
        term = contract_rows(train_feats, resp_rows)
        return (packed, gathered, term, rdiff)

    norm_first = solver_total(jnp.sum(gradient * gradient))
    packed_first, gathered_first, local_first, rdiff_first = apply_curvature(gradient)
    product_first = lax.psum_scatter(
        local_first.astype(jnp.bfloat16), "dp", scatter_dimension=0, tiled=True
    ).astype(jnp.float32)
    curv_first = (
        solver_total(jnp.sum(packed_first.astype(jnp.float32) * product_first))
        + DAMPING * norm_first
    )
    alpha_first = norm_first / curv_first
    residual_next = gradient - alpha_first * (product_first + DAMPING * gradient)
    norm_next = solver_total(jnp.sum(residual_next * residual_next))
    direction_next = residual_next + norm_next / norm_first * gradient
    packed_next, gathered_next, local_next, rdiff_next = apply_curvature(direction_next)
    damped_part = DAMPING * jnp.sum(direction_next * direction_next)
    product_next = lax.psum_scatter(
        local_next.astype(jnp.bfloat16), "dp", scatter_dimension=0, tiled=True
    ).astype(jnp.float32)
    inner_part = jnp.sum(packed_next.astype(jnp.float32) * product_next) + damped_part
    curv_next = solver_total(inner_part)
    alpha_next = norm_next / curv_next
    solution = alpha_first * gradient + alpha_next * direction_next
    influence = -slope_train * (alpha_first * rdiff_first + alpha_next * rdiff_next)
    return (solution, influence)


def solution(mesh):
    placed = (
        P("dp", "fsdp"),
        P("dp", None),
        P("dp"),
        P("dp", None),
        P("dp"),
        P(None, "fsdp"),
        P(None, "fsdp"),
        P("fsdp"),
    )
    return jax.shard_map(
        local, mesh=mesh, in_specs=placed, out_specs=(P("dp", "fsdp"), P("dp")), check_vma=False
    )
```

profile of v0, /device:TPU:1, one launch (start us, length us, event | category | flops | bytes accessed | tf_op | source)
XLA Modules:
  0.0 815.9 jit_solution(4647815058639752397)
XLA Ops:
  7.2 0.0 copy-start
  7.2 0.0 all-gather.5.cloned.1.call-start
  7.2 0.8 slice_bitcast_fusion.3
  8.0 0.8 slice_bitcast_fusion.1
  8.7 0.1 fusion.33
  8.8 0.0 copy-done
  8.8 2.0 gather_fusion
  10.8 0.1 compare_and_fusion
  10.9 0.8 broadcast_select_fusion
  11.7 0.0 all-gather.5.cloned.1.call-update
  11.7 0.0 copy-start.6
  11.7 0.0 all-gather.7.cloned.1.call-start
  11.8 53.5 %all-gather.5.cloned.1.call-done = bf16[272,8192]{1,0:T(8,128)(2,1)} async-done(((bf16[272,256]{1,0:T(8,128)(2,1)}), bf16[272,8192]{1,0:T(8,128)(2,1)}) %all-gather.5.cloned.1.call-update) | async-done | bytes 4456464 | tf_op jit(solution)/shard_map/all_gather | solution.py:35
  65.2 5.5 fusion.17
  70.8 0.0 all-gather.7.cloned.1.call-update
  70.8 0.0 reduce-scatter.5.cloned.1.call-start
  70.8 49.4 %all-gather.7.cloned.1.call-done = bf16[272,8192]{1,0:T(8,128)(2,1)} async-done(((bf16[272,256]{1,0:T(8,128)(2,1)}), bf16[272,8192]{1,0:T(8,128)(2,1)}) %all-gather.7.cloned.1.call-update) | async-done | bytes 4456464 | tf_op jit(solution)/shard_map/all_gather | solution.py:40
  120.2 0.0 copy-done.6
  120.2 5.1 multiply_reduce_fusion.3
  125.4 0.0 copy-done.4
  125.4 3.5 convolution_convert_fusion
  128.8 0.0 reduce-scatter.5.cloned.1.call-update
  128.8 0.0 reduce-scatter.7.cloned.1.call-start
  128.9 62.7 %psum.49 = f32[272]{0:T(512)S(1)} all-reduce(f32[272]{0:T(512)S(1)} %get-tuple-element.23), channel_id=1, replica_groups=mesh['dp'=4,'fsdp'=32] {'fsdp'}, use_global_device_ids=true, to_apply=%region_1.2 | all-reduce | flops 272 | bytes 2176 | tf_op jit(solution)/shard_map/psum | solution.py:45
  191.6 0.0 copy-done.8
  191.6 0.1 fusion.37
  191.7 0.1 pad_maximum_fusion.2
  191.7 18.3 %reduce-scatter.5.cloned.1.call-done = bf16[272,256]{1,0:T(8,128)(2,1)} async-done(((bf16[272,8192]{1,0:T(8,128)(2,1)}), bf16[272,256]{1,0:T(8,128)(2,1)}) %reduce-scatter.5.cloned.1.call-update) | async-done | bytes 139280 | tf_op jit(solution)/shard_map/reduce_scatter | solution.py:50
  210.1 0.0 copy-done.5
  210.1 1.0 convert_multiply_fusion.5
  211.0 4.2 convolution_convert_fusion.3
  215.3 0.0 reduce-scatter.7.cloned.1.call-update
  215.3 0.0 all-gather.9.cloned.1.call-start
  215.3 48.5 %reduce-scatter.7.cloned.1.call-done = bf16[2048,256]{1,0:T(8,128)(2,1)} async-done(((bf16[8192,256]{1,0:T(8,128)(2,1)}), bf16[2048,256]{1,0:T(8,128)(2,1)}) %reduce-scatter.7.cloned.1.call-update) | async-done | bytes 1048592 | tf_op jit(solution)/shard_map/reduce_scatter | solution.py:62
  263.8 0.0 all-gather.9.cloned.1.call-update
  263.9 0.0 copy-start.7
  263.9 0.0 reduce-scatter.9.cloned.1.call-start
  263.9 49.5 %all-gather.9.cloned.1.call-done = bf16[8192,256]{1,0:T(8,128)(2,1)} async-done(((bf16[2048,256]{1,0:T(8,128)(2,1)}), bf16[8192,256]{1,0:T(8,128)(2,1)}) %all-gather.9.cloned.1.call-update) | async-done | bytes 4194320 | tf_op jit(solution)/shard_map/all_gather | solution.py:70
  313.4 4.8 fusion.22
  318.2 62.7 %psum.51 = f32[256]{0:T(256)S(1)} all-reduce(f32[256]{0:T(256)S(1)} %fusion.22), channel_id=1, replica_groups=mesh['dp'=4,'fsdp'=32] {'fsdp'}, use_global_device_ids=true, to_apply=%region_7.8 | all-reduce | flops 256 | bytes 2048 | tf_op jit(solution)/shard_map/psum | solution.py:72
  380.9 0.0 copy-done.7
  380.9 5.5 convolution_convert_fusion.2
  386.4 0.0 reduce-scatter.9.cloned.1.call-update
  386.5 0.0 all-gather.11.cloned.1.call-start
  386.5 46.8 %reduce-scatter.9.cloned.1.call-done = bf16[2048,256]{1,0:T(8,128)(2,1)} async-done(((bf16[8192,256]{1,0:T(8,128)(2,1)}), bf16[2048,256]{1,0:T(8,128)(2,1)}) %reduce-scatter.9.cloned.1.call-update) | async-done | bytes 1048592 | tf_op jit(solution)/shard_map/reduce_scatter | solution.py:81
  433.3 0.0 copy-done.1
  433.3 2.5 fusion.8
  435.8 64.6 %all-reduce = (f32[]{:T(128)}, f32[]{:T(128)}) all-reduce(f32[]{:T(128)} %get-tuple-element.3, f32[]{:T(128)} %get-tuple-element.2), channel_id=1, replica_groups=mesh['dp'=4,'fsdp'=32] {'dp','fsdp'}, use_global_device_ids=true, to_apply=%region_5.6 | all-reduce | flops 2 | bytes 16 | tf_op jit(solution)/shard_map/psum | solution.py:18
  502.3 2.4 multiply_reduce_fusion.2
  504.7 64.3 %psum.53 = f32[]{:T(128)} all-reduce(f32[]{:T(128)} %multiply_reduce_fusion.2), channel_id=1, replica_groups=mesh['dp'=4,'fsdp'=32] {'dp','fsdp'}, use_global_device_ids=true, to_apply=%region_12.13 | all-reduce | flops 1 | bytes 8 | tf_op jit(solution)/shard_map/psum | solution.py:18
  570.4 0.0 copy-done.2
  570.4 2.3 multiply_reduce_fusion
  572.7 0.0 all-gather.11.cloned.1.call-update
  572.7 0.0 reduce-scatter.11.cloned.1.call-start
  572.7 45.0 %all-gather.11.cloned.1.call-done = bf16[8192,256]{1,0:T(8,128)(2,1)} async-done(((bf16[2048,256]{1,0:T(8,128)(2,1)}), bf16[8192,256]{1,0:T(8,128)(2,1)}) %all-gather.11.cloned.1.call-update) | async-done | bytes 4194320 | tf_op jit(solution)/shard_map/all_gather | solution.py:70
  617.7 4.8 fusion.19
  622.5 62.7 %psum.54 = f32[256]{0:T(256)S(1)} all-reduce(f32[256]{0:T(256)S(1)} %fusion.19), channel_id=1, replica_groups=mesh['dp'=4,'fsdp'=32] {'fsdp'}, use_global_device_ids=true, to_apply=%region_14.15 | all-reduce | flops 256 | bytes 2048 | tf_op jit(solution)/shard_map/psum | solution.py:72
  685.2 5.5 convolution_convert_fusion.1
  690.7 0.0 reduce-scatter.11.cloned.1.call-update
  691.5 46.1 %reduce-scatter.11.cloned.1.call-done = bf16[2048,256]{1,0:T(8,128)(2,1)} async-done(((bf16[8192,256]{1,0:T(8,128)(2,1)}), bf16[2048,256]{1,0:T(8,128)(2,1)}) %reduce-scatter.11.cloned.1.call-update) | async-done | bytes 1048592 | tf_op jit(solution)/shard_map/reduce_scatter | solution.py:94
  737.6 2.4 multiply_reduce_fusion.1
  740.6 64.5 %psum.55 = f32[]{:T(128)} all-reduce(f32[]{:T(128)S(6)} %add.83), channel_id=1, replica_groups=mesh['dp'=4,'fsdp'=32] {'dp','fsdp'}, use_global_device_ids=true, to_apply=%region_18.19 | all-reduce | flops 1 | bytes 8 | tf_op jit(solution)/shard_map/psum | solution.py:18
  806.5 0.5 add_multiply_fusion
  807.0 2.1 fusion.9
  (13 shorter events, 0.1 us)
Async XLA Ops:
  7.2 1.7 copy-start
  7.2 58.0 %all-gather.5.cloned.1.call-start = ((), (), s32[]{:S(2)}) async-start(), calls=%async_computation.4 | async-start | bytes 4595712 | tf_op jit(solution)/shard_map/all_gather | solution.py:35
  11.7 108.5 %copy-start.6 = (f32[256]{0:T(256)S(1)}, f32[256]{0:T(256)}, u32[]{:S(2)}) copy-start(f32[256]{0:T(256)} %param.15) | copy-start | bytes 3076
  11.7 108.5 %all-gather.7.cloned.1.call-start = ((), (), s32[]{:S(2)}) async-start(), calls=%async_computation.5 | async-start | bytes 4595712 | tf_op jit(solution)/shard_map/all_gather | solution.py:40
  70.8 139.3 %reduce-scatter.5.cloned.1.call-start = ((), (), s32[]{:S(2)}) async-start(), calls=%async_computation.6 | async-start | bytes 4595712 | tf_op jit(solution)/shard_map/reduce_scatter | solution.py:50
  120.2 5.1 copy-start.4
  128.8 62.8 %copy-start.8 = (s32[8]{0:T(128)S(1)}, s32[8]{0:T(128)}, u32[]{:S(2)}) copy-start(s32[8]{0:T(128)} %param.12) | copy-start | bytes 100
  128.8 81.3 %copy-start.5 = (bf16[272,256]{1,0:T(8,128)(2,1)S(1)}, bf16[272,256]{1,0:T(8,128)(2,1)}, u32[]{:S(2)}) copy-start(bf16[272,256]{1,0:T(8,128)(2,1)} %fusion.17) | copy-start | bytes 417796
  128.8 135.0 %reduce-scatter.7.cloned.1.call-start = ((), (), s32[]{:S(2)}) async-start(), calls=%async_computation.7 | async-start | bytes 5242880 | tf_op jit(solution)/shard_map/reduce_scatter | solution.py:62
  215.3 98.1 %all-gather.9.cloned.1.call-start = ((), (), s32[]{:S(2)}) async-start(), calls=%async_computation.8 | async-start | bytes 5242880 | tf_op jit(solution)/shard_map/all_gather | solution.py:70
  263.9 117.0 %copy-start.7 = (s32[128]{0:T(128)S(1)}, s32[128]{0:T(128)}, u32[]{:S(2)}) copy-start(s32[128]{0:T(128)} %param.10) | copy-start | bytes 1540
  263.9 169.4 %reduce-scatter.9.cloned.1.call-start = ((), (), s32[]{:S(2)}) async-start(), calls=%async_computation.9 | async-start | bytes 5242880 | tf_op jit(solution)/shard_map/reduce_scatter | solution.py:81
  386.4 46.9 %copy-start.1 = (bf16[2048,256]{1,0:T(8,128)(2,1)S(1)}, bf16[2048,256]{1,0:T(8,128)(2,1)}, u32[]{:S(2)}) copy-start(bf16[2048,256]{1,0:T(8,128)(2,1)} %reduce-scatter.7.cloned.1.call-done) | copy-start | bytes 3145732
  386.5 231.2 %all-gather.11.cloned.1.call-start = ((), (), s32[]{:S(2)}) async-start(), calls=%async_computation.10 | async-start | bytes 5242880 | tf_op jit(solution)/shard_map/all_gather | solution.py:70
  433.3 137.1 %copy-start.2 = (bf16[2048,256]{1,0:T(8,128)(2,1)S(1)}, bf16[2048,256]{1,0:T(8,128)(2,1)}, u32[]{:S(2)}) copy-start(bf16[2048,256]{1,0:T(8,128)(2,1)} %reduce-scatter.9.cloned.1.call-done) | copy-start | bytes 3145732
  572.7 164.9 %reduce-scatter.11.cloned.1.call-start = ((), (), s32[]{:S(2)}) async-start(), calls=%async_computation.11 | async-start | bytes 5242880 | tf_op jit(solution)/shard_map/reduce_scatter | solution.py:94
  690.7 46.9 %copy-start.3 = (bf16[2048,256]{1,0:T(8,128)(2,1)S(1)}, bf16[2048,256]{1,0:T(8,128)(2,1)}, u32[]{:S(2)}) copy-start(bf16[2048,256]{1,0:T(8,128)(2,1)} %get-tuple-element.12) | copy-start | bytes 3145732
Sparse Core Ops, SparseCore 0:
  11.8 53.3 all-gather.4
  70.9 49.2 all-gather.6
  129.0 81.0 reduce-scatter.4
  215.4 48.3 reduce-scatter.6
  265.4 47.9 all-gather.8
  386.6 46.6 reduce-scatter.8
  572.8 44.8 all-gather.10
  690.9 46.6 reduce-scatter.10
where the time goes:
time: 817 us; the launch traced here: 816 us
  blocking collectives  381 us (47%)
  waiting for transfers between devices  357 us (44%)
  matrix products  38.9 us (5%)
  between operations  20.2 us (2%)
  other arithmetic  14.2 us (2%)
    psum x3, blocking collectives, solver_total(): return lax.psum(value, ('dp', 'fsdp'))  193 us
    psum x2, blocking collectives, apply_curvature(): response = lax.psum(jnp.sum(train_mix * project, axis=1), 'fsdp')  125 us
    all_gather x2, waiting for transfers between devices, apply_curvature(): gathered = lax.all_gather(packed, 'dp', axis=0, tiled=True)  94.4 us
    psum x1, blocking collectives, local(): scores_all = lax.psum(jnp.sum(output_act * head_weight, axis=1), 'fsdp')  62.7 us
    all_gather x1, waiting for transfers between devices, local(): feats = lax.all_gather(local_rows, 'fsdp', axis=1, tiled=True)  53.5 us
    all_gather x1, waiting for transfers between devices, local(): lax.all_gather(hidden, 'fsdp', axis=1, tiled=True)  49.4 us
    reduce_scatter x1, waiting for transfers between devices, local(): lax.psum_scatter(grad_local.astype(jnp.bfloat16), 'dp', scatter_dimension...  48.5 us
    reduce_scatter x1, waiting for transfers between devices, local(): lax.psum_scatter(local_first.astype(jnp.bfloat16), 'dp', scatter_dimensio...  46.8 us
  transfers between devices with their start and end apart: 8, of which 8 were waited for; matrix products, arithmetic and copies ran while one was open for 0% of the time, Pallas kernels for 0%

commit v1 on v0

--- a/solution.py
+++ b/solution.py
@@ -15,7 +15,7 @@
 
 
 def solver_total(value):
-    return lax.psum(value, ("dp", "fsdp"))
+    return lax.psum(lax.psum(value, "dp"), "fsdp")
 
 
 def contract_rows(left, right):

time: 817 us -> 842 us (1.031)
  blocking collectives: 381 us -> 408 us
    psum x3 -> x6, blocking collectives: 193 us -> 220 us  [solver_total(): return lax.psum(lax.psum(value, 'dp'), 'fsdp')]
where the time goes in v1:
time: 842 us; the launch traced here: 840 us
  blocking collectives  408 us (48%)
  waiting for transfers between devices  355 us (42%)
  matrix products  38.9 us (5%)
  between operations  20.2 us (2%)
  other arithmetic  14.2 us (2%)
    psum x6, blocking collectives, solver_total(): return lax.psum(lax.psum(value, 'dp'), 'fsdp')  220 us
    psum x2, blocking collectives, apply_curvature(): response = lax.psum(jnp.sum(train_mix * project, axis=1), 'fsdp')  125 us
    all_gather x2, waiting for transfers between devices, apply_curvature(): gathered = lax.all_gather(packed, 'dp', axis=0, tiled=True)  92 us
    psum x1, blocking collectives, local(): scores_all = lax.psum(jnp.sum(output_act * head_weight, axis=1), 'fsdp')  62.7 us
    all_gather x1, waiting for transfers between devices, local(): feats = lax.all_gather(local_rows, 'fsdp', axis=1, tiled=True)  53.5 us
    all_gather x1, waiting for transfers between devices, local(): lax.all_gather(hidden, 'fsdp', axis=1, tiled=True)  49.4 us
    reduce_scatter x1, waiting for transfers between devices, local(): lax.psum_scatter(grad_local.astype(jnp.bfloat16), 'dp', scatter_dimension...  48.5 us
    reduce_scatter x1, waiting for transfers between devices, local(): lax.psum_scatter(local_first.astype(jnp.bfloat16), 'dp', scatter_dimensio...  46.8 us
  transfers between devices with their start and end apart: 8, of which 8 were waited for; matrix products, arithmetic and copies ran while one was open for 0% of the time, Pallas kernels for 0%

profile of v1, /device:TPU:1, one launch (start us, length us, event | category | flops | bytes accessed | tf_op | source)
XLA Modules:
  0.0 840.0 jit_solution(15321745633866801620)
XLA Ops:
  7.2 0.0 copy-start
  7.2 0.0 all-gather.5.cloned.1.call-start
  7.2 0.8 slice_bitcast_fusion.3
  8.0 0.8 slice_bitcast_fusion.1
  8.7 0.1 fusion.33
  8.8 0.0 copy-done
  8.8 2.0 gather_fusion
  10.8 0.1 compare_and_fusion
  10.9 0.8 broadcast_select_fusion
  11.7 0.0 all-gather.5.cloned.1.call-update
  11.7 0.0 copy-start.6
  11.7 0.0 all-gather.7.cloned.1.call-start
  11.8 53.5 %all-gather.5.cloned.1.call-done = bf16[272,8192]{1,0:T(8,128)(2,1)} async-done(((bf16[272,256]{1,0:T(8,128)(2,1)}), bf16[272,8192]{1,0:T(8,128)(2,1)}) %all-gather.5.cloned.1.call-update) | async-done | bytes 4456464 | tf_op jit(solution)/shard_map/all_gather | solution.py:35
  65.2 5.5 fusion.17
  70.8 0.0 all-gather.7.cloned.1.call-update
  70.8 0.0 reduce-scatter.5.cloned.1.call-start
  70.8 49.4 %all-gather.7.cloned.1.call-done = bf16[272,8192]{1,0:T(8,128)(2,1)} async-done(((bf16[272,256]{1,0:T(8,128)(2,1)}), bf16[272,8192]{1,0:T(8,128)(2,1)}) %all-gather.7.cloned.1.call-update) | async-done | bytes 4456464 | tf_op jit(solution)/shard_map/all_gather | solution.py:40
  120.2 0.0 copy-done.6
  120.2 5.1 multiply_reduce_fusion.3
  125.4 0.0 copy-done.4
  125.4 3.5 convolution_convert_fusion
  128.8 0.0 reduce-scatter.5.cloned.1.call-update
  128.8 0.0 reduce-scatter.7.cloned.1.call-start
  128.9 62.7 %psum.77 = f32[272]{0:T(512)S(1)} all-reduce(f32[272]{0:T(512)S(1)} %get-tuple-element.25), channel_id=1, replica_groups=mesh['dp'=4,'fsdp'=32] {'fsdp'}, use_global_device_ids=true, to_apply=%region_1.2 | all-reduce | flops 272 | bytes 2176 | tf_op jit(solution)/shard_map/psum | solution.py:45
  191.6 0.0 copy-done.8
  191.6 0.1 fusion.37
  191.7 0.1 pad_maximum_fusion.2
  191.7 18.3 %reduce-scatter.5.cloned.1.call-done = bf16[272,256]{1,0:T(8,128)(2,1)} async-done(((bf16[272,8192]{1,0:T(8,128)(2,1)}), bf16[272,256]{1,0:T(8,128)(2,1)}) %reduce-scatter.5.cloned.1.call-update) | async-done | bytes 139280 | tf_op jit(solution)/shard_map/reduce_scatter | solution.py:50
  210.1 0.0 copy-done.5
  210.1 1.0 convert_multiply_fusion.5
  211.0 4.2 convolution_convert_fusion.3
  215.3 0.0 reduce-scatter.7.cloned.1.call-update
  215.3 0.0 all-gather.9.cloned.1.call-start
  215.3 48.5 %reduce-scatter.7.cloned.1.call-done = bf16[2048,256]{1,0:T(8,128)(2,1)} async-done(((bf16[8192,256]{1,0:T(8,128)(2,1)}), bf16[2048,256]{1,0:T(8,128)(2,1)}) %reduce-scatter.7.cloned.1.call-update) | async-done | bytes 1048592 | tf_op jit(solution)/shard_map/reduce_scatter | solution.py:62
  263.8 0.0 all-gather.9.cloned.1.call-update
  263.9 0.0 copy-start.7
  263.9 0.0 reduce-scatter.9.cloned.1.call-start
  263.9 49.5 %all-gather.9.cloned.1.call-done = bf16[8192,256]{1,0:T(8,128)(2,1)} async-done(((bf16[2048,256]{1,0:T(8,128)(2,1)}), bf16[8192,256]{1,0:T(8,128)(2,1)}) %all-gather.9.cloned.1.call-update) | async-done | bytes 4194320 | tf_op jit(solution)/shard_map/all_gather | solution.py:70
  313.4 4.8 fusion.22
  318.2 62.7 %psum.80 = f32[256]{0:T(256)S(1)} all-reduce(f32[256]{0:T(256)S(1)} %fusion.22), channel_id=1, replica_groups=mesh['dp'=4,'fsdp'=32] {'fsdp'}, use_global_device_ids=true, to_apply=%region_8.9 | all-reduce | flops 256 | bytes 2048 | tf_op jit(solution)/shard_map/psum | solution.py:72
  380.9 5.5 convolution_convert_fusion.2
  386.4 0.0 reduce-scatter.9.cloned.1.call-update
  386.5 0.0 all-gather.11.cloned.1.call-start
  386.5 46.8 %reduce-scatter.9.cloned.1.call-done = bf16[2048,256]{1,0:T(8,128)(2,1)} async-done(((bf16[8192,256]{1,0:T(8,128)(2,1)}), bf16[2048,256]{1,0:T(8,128)(2,1)}) %reduce-scatter.9.cloned.1.call-update) | async-done | bytes 1048592 | tf_op jit(solution)/shard_map/reduce_scatter | solution.py:81
  433.3 2.5 fusion.8
  435.8 7.1 all-reduce.1
  442.9 65.3 %all-reduce = (f32[]{:T(128)}, f32[]{:T(128)}) all-reduce(f32[]{:T(128)} %get-tuple-element.6, f32[]{:T(128)} %get-tuple-element.7), channel_id=1, replica_groups=mesh['dp'=4,'fsdp'=32] {'fsdp'}, use_global_device_ids=true, to_apply=%region_6.7 | all-reduce | flops 2 | bytes 16 | tf_op jit(solution)/shard_map/psum | solution.py:18
  510.1 2.4 multiply_reduce_fusion.2
  512.5 7.6 psum.83
  520.0 67.6 %psum.84 = f32[]{:T(128)} all-reduce(f32[]{:T(128)} %psum.83), channel_id=1, replica_groups=mesh['dp'=4,'fsdp'=32] {'fsdp'}, use_global_device_ids=true, to_apply=%region_15.16 | all-reduce | flops 1 | bytes 8 | tf_op jit(solution)/shard_map/psum | solution.py:18
  589.0 2.3 multiply_reduce_fusion
  591.3 0.0 all-gather.11.cloned.1.call-update
  591.4 0.2 reduce-scatter.11.cloned.1.call-start
  591.6 42.5 %all-gather.11.cloned.1.call-done = bf16[8192,256]{1,0:T(8,128)(2,1)} async-done(((bf16[2048,256]{1,0:T(8,128)(2,1)}), bf16[8192,256]{1,0:T(8,128)(2,1)}) %all-gather.11.cloned.1.call-update) | async-done | bytes 4194320 | tf_op jit(solution)/shard_map/all_gather | solution.py:70
  634.1 4.8 fusion.19
  638.9 62.7 %psum.85 = f32[256]{0:T(256)S(1)} all-reduce(f32[256]{0:T(256)S(1)} %fusion.19), channel_id=1, replica_groups=mesh['dp'=4,'fsdp'=32] {'fsdp'}, use_global_device_ids=true, to_apply=%region_17.18 | all-reduce | flops 256 | bytes 2048 | tf_op jit(solution)/shard_map/psum | solution.py:72
  701.6 5.5 convolution_convert_fusion.1
  707.1 0.0 reduce-scatter.11.cloned.1.call-update
  707.8 46.1 %reduce-scatter.11.cloned.1.call-done = bf16[2048,256]{1,0:T(8,128)(2,1)} async-done(((bf16[8192,256]{1,0:T(8,128)(2,1)}), bf16[2048,256]{1,0:T(8,128)(2,1)}) %reduce-scatter.11.cloned.1.call-update) | async-done | bytes 1048592 | tf_op jit(solution)/shard_map/reduce_scatter | solution.py:94
  754.0 2.4 multiply_reduce_fusion.1
  757.0 7.0 psum.86
  764.0 65.3 %psum.87 = f32[]{:T(128)} all-reduce(f32[]{:T(128)} %psum.86), channel_id=1, replica_groups=mesh['dp'=4,'fsdp'=32] {'fsdp'}, use_global_device_ids=true, to_apply=%region_22.23 | all-reduce | flops 1 | bytes 8 | tf_op jit(solution)/shard_map/psum | solution.py:18
  830.6 0.5 add_multiply_fusion
  831.1 2.1 fusion.9
  (16 shorter events, 0.1 us)
Async XLA Ops:
  7.2 1.7 copy-start
  7.2 58.0 %all-gather.5.cloned.1.call-start = ((), (), s32[]{:S(2)}) async-start(), calls=%async_computation.4 | async-start | bytes 4595712 | tf_op jit(solution)/shard_map/all_gather | solution.py:35
  11.7 108.5 %copy-start.6 = (f32[256]{0:T(256)S(1)}, f32[256]{0:T(256)}, u32[]{:S(2)}) copy-start(f32[256]{0:T(256)} %param.15) | copy-start | bytes 3076
  11.7 108.5 %all-gather.7.cloned.1.call-start = ((), (), s32[]{:S(2)}) async-start(), calls=%async_computation.5 | async-start | bytes 4595712 | tf_op jit(solution)/shard_map/all_gather | solution.py:40
  70.8 139.3 %reduce-scatter.5.cloned.1.call-start = ((), (), s32[]{:S(2)}) async-start(), calls=%async_computation.6 | async-start | bytes 4595712 | tf_op jit(solution)/shard_map/reduce_scatter | solution.py:50
  120.2 5.1 copy-start.4
  128.8 62.8 %copy-start.8 = (s32[8]{0:T(128)S(1)}, s32[8]{0:T(128)}, u32[]{:S(2)}) copy-start(s32[8]{0:T(128)} %param.12) | copy-start | bytes 100
  128.8 81.3 %copy-start.5 = (bf16[272,256]{1,0:T(8,128)(2,1)S(1)}, bf16[272,256]{1,0:T(8,128)(2,1)}, u32[]{:S(2)}) copy-start(bf16[272,256]{1,0:T(8,128)(2,1)} %fusion.17) | copy-start | bytes 417796
  128.8 135.0 %reduce-scatter.7.cloned.1.call-start = ((), (), s32[]{:S(2)}) async-start(), calls=%async_computation.7 | async-start | bytes 5242880 | tf_op jit(solution)/shard_map/reduce_scatter | solution.py:62
  215.3 98.1 %all-gather.9.cloned.1.call-start = ((), (), s32[]{:S(2)}) async-start(), calls=%async_computation.8 | async-start | bytes 5242880 | tf_op jit(solution)/shard_map/all_gather | solution.py:70
  263.9 117.0 %copy-start.7 = (s32[128]{0:T(128)S(1)}, s32[128]{0:T(128)}, u32[]{:S(2)}) copy-start(s32[128]{0:T(128)} %param.10) | copy-start | bytes 1540
  263.9 169.4 %reduce-scatter.9.cloned.1.call-start = ((), (), s32[]{:S(2)}) async-start(), calls=%async_computation.9 | async-start | bytes 5242880 | tf_op jit(solution)/shard_map/reduce_scatter | solution.py:81
  386.4 46.9 %copy-start.1 = (bf16[2048,256]{1,0:T(8,128)(2,1)S(1)}, bf16[2048,256]{1,0:T(8,128)(2,1)}, u32[]{:S(2)}) copy-start(bf16[2048,256]{1,0:T(8,128)(2,1)} %reduce-scatter.7.cloned.1.call-done) | copy-start | bytes 3145732
  386.5 247.6 %all-gather.11.cloned.1.call-start = ((), (), s32[]{:S(2)}) async-start(), calls=%async_computation.10 | async-start | bytes 5242880 | tf_op jit(solution)/shard_map/all_gather | solution.py:70
  433.3 155.7 %copy-start.2 = (bf16[2048,256]{1,0:T(8,128)(2,1)S(1)}, bf16[2048,256]{1,0:T(8,128)(2,1)}, u32[]{:S(2)}) copy-start(bf16[2048,256]{1,0:T(8,128)(2,1)} %reduce-scatter.9.cloned.1.call-done) | copy-start | bytes 3145732
  591.4 162.6 %reduce-scatter.11.cloned.1.call-start = ((), (), s32[]{:S(2)}) async-start(), calls=%async_computation.11 | async-start | bytes 5242880 | tf_op jit(solution)/shard_map/reduce_scatter | solution.py:94
  707.1 46.9 %copy-start.3 = (bf16[2048,256]{1,0:T(8,128)(2,1)S(1)}, bf16[2048,256]{1,0:T(8,128)(2,1)}, u32[]{:S(2)}) copy-start(bf16[2048,256]{1,0:T(8,128)(2,1)} %get-tuple-element.14) | copy-start | bytes 3145732
Sparse Core Ops, SparseCore 0:
  11.8 53.3 all-gather.4
  70.9 49.2 all-gather.6
  129.0 81.0 reduce-scatter.4
  215.4 48.3 reduce-scatter.6
  265.4 47.9 all-gather.8
  386.6 46.6 reduce-scatter.8
  591.5 42.5 all-gather.10
  707.3 46.6 reduce-scatter.10
